TPU v7x, 32 devices: a whole 2x2x4 slice. The times are simulated.
32 devices in a mesh: grp: 2 (over x), lat: 8 (over z, y), lon: 2 (over core).
Axes of the slice: x: 2, y: 2, z: 4, core: 2. Of those that a mesh axis runs over, the one named last changes fastest.
Arguments:
- perturb: float32 [256, 256, 192], P(('grp', 'lat'), 'lon'), parts along dimension 0, may hold values from -110 to 110, as said below
- kernels: float32 [2, 7, 7, 192], replicated, may hold values from -0.875 to 0.875
- gains: float32 [2, 192], replicated, may hold values from 0.5 to 1.5
- w_in: bfloat16 [2, 192, 768], replicated, may hold values from -0.4375 to 0.4375
- w_out: bfloat16 [2, 768, 192], replicated, may hold values from -0.21875 to 0.21875
- scales: float32 [2, 192], replicated, may hold values from 0.3 to 1.5
- normed: bfloat16 [2, 256, 256, 192], P(None, ('grp', 'lat'), 'lon'), parts along dimension 1, may hold values from -6 to 6
- inv_std: float32 [2, 256, 256], P(None, ('grp', 'lat'), 'lon'), parts along dimension 1, may hold values from 0.5 to 2
- slope: bfloat16 [2, 256, 256, 768], P(None, ('grp', 'lat'), 'lon'), parts along dimension 1, may hold values from -0.099609375 to 1.09375
Outputs:
- new_vec: float32 [256, 256, 192], P(('grp', 'lat'), 'lon'), parts along dimension 0
- growth: float32 [2], P('grp'), parts along dimension 0
There are 2 independent parts, one for each index of `grp`. A program takes and returns all parts, laid end to end along the dimension named above; an argument that names none is the same for every part. Nothing has to cross between parts.
Inputs may be any that keep to these rules, and one draw needn't show every extreme that they name: `perturb`: the initial perturbation.
All inputs are finite; a program needn't handle non-finite values.
Results may differ from a plain program's by a relative error of at most 0.0075.
Values may be sent and summed in bfloat16 or wider, within the bound.
No kernel may reach another device: no remote copies, remote signals or barrier semaphores. Data moves between devices by JAX's collectives and lax.ppermute only.
A program may use at most 64 MiB of HBM per device.

v0:
```python
import math
import jax
import jax.numpy as jnp
from jax import lax
from jax.sharding import PartitionSpec as P

lat_span = 70.0 * math.pi / 180.0


def extended(x, sides, width, wrap):
    for axis, dim in sides:
        size, length = (lax.axis_size(axis), x.shape[dim])
        up = [(i, (i + 1) % size) for i in range(size if wrap else size - 1)]
        down = [(j, i) for i, j in up]
        last = lax.slice_in_dim(x, length - width, length, axis=dim)
        initial = lax.slice_in_dim(x, 0, width, axis=dim)
        before = lax.ppermute(last, axis, up)
        after = lax.ppermute(initial, axis, down)
        x = jnp.concatenate([before, x, after], axis=dim)
    return x


def tangent_pad(rounded):
    widened = extended(rounded, (("lon", 1),), 3, True)
    return extended(widened, (("lat", 0),), 3, False)


def adjoint_pad(rounded):
    widened = extended(rounded, (("lon", 1),), 3, True)
    return extended(widened, (("lat", 0),), 3, False)


def window_sum(padded, kernel, row_count, col_count, flipped):
    summed = jnp.zeros((row_count, col_count, padded.shape[2]), jnp.float32)
    for row_off in range(7):
        for col_off in range(7):
            row_start = 6 - row_off if flipped else row_off
            col_start = 6 - col_off if flipped else col_off
            window_part = padded[
                row_start : row_start + row_count, col_start : col_start + col_count
            ].astype(jnp.float32)
            summed = summed + kernel[row_off, col_off] * window_part
    return summed


def project(values, normed_layer, inv_layer):
    normal_f = normed_layer.astype(jnp.float32)
    centred = (
        values
        - jnp.mean(values, axis=-1, keepdims=True)
        - normal_f * jnp.mean(normal_f * values, axis=-1, keepdims=True)
    )
    return inv_layer[..., None] * centred


def on_device(perturb, kernels, gains, w_in, w_out, scales, normed, inv_std, slope):
    row_count, col_count, chans = perturb.shape
    lat_total = row_count * lax.axis_size("lat")
    lon_total = col_count * lax.axis_size("lon")
    local_rows = (lax.axis_index("lat") * row_count + jnp.arange(row_count)).astype(jnp.float32)
    area_rows = jnp.cos(lat_span * (local_rows + 0.5) / lat_total)
    area_w = area_rows[:, None, None]
    every_row = jnp.arange(lat_total).astype(jnp.float32)
    weight_total = jnp.sum(jnp.cos(lat_span * (every_row + 0.5) / lat_total)) * lon_total * chans
    layer_count = kernels.shape[0]
    tangent = perturb
    for layer_index in range(layer_count):
        rounded = tangent.astype(jnp.bfloat16)
        padded = tangent_pad(rounded)
        conv_out = window_sum(padded, kernels[layer_index], row_count, col_count, False)
        tangent_norm = project(conv_out, normed[layer_index], inv_std[layer_index])
        operand = (gains[layer_index] * tangent_norm).astype(jnp.bfloat16)
        hidden_pre = jnp.dot(operand, w_in[layer_index], preferred_element_type=jnp.float32)
        gated = (slope[layer_index] * hidden_pre).astype(jnp.bfloat16)
        branch_out = jnp.dot(gated, w_out[layer_index], preferred_element_type=jnp.float32)
        tangent = tangent + scales[layer_index] * branch_out
    start_local = jnp.sum(area_w * perturb * perturb)
    forward_local = jnp.sum(area_w * tangent * tangent)
    grad_field = area_w * tangent
    for layer_index in range(layer_count - 1, -1, -1):
        scaled = (scales[layer_index] * grad_field).astype(jnp.bfloat16)
        hidden_back = lax.dot_general(
            scaled, w_out[layer_index], (((2,), (1,)), ((), ())), preferred_element_type=jnp.float32
        )
        gated = (slope[layer_index] * hidden_back).astype(jnp.bfloat16)
        chan_back = lax.dot_general(
            gated, w_in[layer_index], (((2,), (1,)), ((), ())), preferred_element_type=jnp.float32
        )
        conv_grad = project(
            gains[layer_index] * chan_back, normed[layer_index], inv_std[layer_index]
        ).astype(jnp.bfloat16)
        padded = adjoint_pad(conv_grad)
        conv_back = window_sum(padded, kernels[layer_index], row_count, col_count, True)
        grad_field = grad_field + conv_back
    adjoint_out = grad_field / area_w
    adjoint_local = jnp.sum(area_w * adjoint_out * adjoint_out)
    start_sum, forward_sum, adjoint_sum = lax.psum(
        (start_local, forward_local, adjoint_local), ("lat", "lon")
    )
    start_sq = start_sum / weight_total
    forward_sq = forward_sum / weight_total
    adjoint_sq = adjoint_sum / weight_total
    growth = jnp.sqrt(forward_sq / (start_sq + 1e-06)).reshape(1)
    new_vec = adjoint_out / jnp.sqrt(adjoint_sq + 1e-06)
    return (new_vec, growth)


def solution(mesh):
    in_specs = (
        P(("grp", "lat"), "lon", None),
        P(),
        P(),
        P(),
        P(),
        P(),
        P(None, ("grp", "lat"), "lon", None),
        P(None, ("grp", "lat"), "lon"),
        P(None, ("grp", "lat"), "lon", None),
    )
    out_specs = (P(("grp", "lat"), "lon", None), P("grp"))
    return jax.shard_map(
        on_device, mesh=mesh, in_specs=in_specs, out_specs=out_specs, check_vma=False
    )
```

profile of v0, /device:TPU:0, one launch (start us, length us, event | category | flops | bytes accessed | tf_op | source)
XLA Modules:
  0.0 238.3 jit_solution(1238597391319515903)
XLA Ops:
  0.6 1.5 convert_element_type.665
  2.2 0.3 fusion.143
  2.5 0.4 copy.14
  2.9 0.5 collective-permute-start
  3.4 0.4 copy.15
  4.5 0.6 fusion.150
  5.1 0.7 fusion.145
  5.8 0.6 fusion.151
  6.4 0.4 copy.16
  6.9 0.4 copy.17
  7.3 0.4 pad_maximum_fusion.23
  7.7 4.9 %collective-permute-start.2 = (bf16[3,134,192]{1,2,0:T(8,128)(2,1)S(1)}, bf16[3,134,192]{1,2,0:T(8,128)(2,1)S(1)}, u32[]{:S(2)}, u32[]{:S(2)}) collective-permute-start(bf16[3,134,192]{1,2,0:T(8,128)(2,1)S(1)} %get-tuple-element.33), channel_id=1, source_target_pairs={{0,2},{2,4},{4,6},{6,8},{8,10},{10,12},{12,14},{1,3},{3,5},{5,7},{... | collective-permute-start | bytes 463112 | tf_op jit(solution)/shard_map/ppermute | solution.py:17
  12.6 1.3 collective-permute-start.3
  13.9 0.6 fusion.152
  14.5 10.8 %collective-permute-done.2 = bf16[3,134,192]{1,2,0:T(8,128)(2,1)S(1)} collective-permute-done((bf16[3,134,192]{1,2,0:T(8,128)(2,1)S(1)}, bf16[3,134,192]{1,2,0:T(8,128)(2,1)S(1)}, u32[]{:S(2)}, u32[]{:S(2)}) %collective-permute-start.2) | collective-permute-done | bytes 154400 | tf_op jit(solution)/shard_map/ppermute | solution.py:17
  25.3 2.2 maximum_maximum_fusion
  28.0 18.3 %fusion.139 = (f32[16,128]{1,0:T(8,128)S(1)}, f32[16,128]{1,0:T(8,128)S(1)}, f32[16,128,192]{1,2,0:T(8,128)}) fusion(bf16[2,16,128,192]{2,3,1,0:T(8,128)(2,1)S(1)} %copy-done.5, bf16[19,134,192]{1,2,0:T(8,128)(2,1)S(1)} %get-tuple-element.32, f32[192]{0:T(256)S(1)} %bitcast.247, f32[192]{0:T(256)S(1)} %bitcast.249, f32[192]{0:T(256)S(1)} %bitcast.251, ...), kind=kLoop, calls=%fused_computation.193 | loop fusion | flops 66056192 | bytes 36266752 | tf_op jit(solution)/shard_map/reduce_sum | solution.py:50
  46.3 6.5 %fusion.153 = (bf16[16,128,192]{1,2,0:T(8,128)(2,1)S(1)}, f32[16,128,192]{1,2,0:T(8,128)}) fusion(f32[16,128,192]{1,2,0:T(8,128)} %param.9, bf16[2,768,192]{1,2,0:T(8,128)(2,1)S(1)} %copy-done.170, bf16[2,16,128,768]{3,2,1,0:T(8,128)(2,1)} %param.17, f32[16,128,192]{1,2,0:T(8,128)} %get-tuple-element.18, f32[16,128]{1,0:T(8,128)S(1)} %broadcast_multiply_fusion.6, ...), kind=kOutput, calls=%fused_computation.207 | convolution fusion | flops 1216610304 | bytes 10053632 | tf_op jit(solution)/shard_map/dot_general | solution.py:75
  53.1 0.4 copy.21
  53.6 0.4 copy.22
  54.0 0.6 collective-permute-start.5
  54.5 0.7 fusion.146
  55.2 0.4 copy.23
  55.6 0.4 copy.24
  56.1 0.4 pad_maximum_fusion.20
  56.4 4.4 %collective-permute-start.6 = (bf16[3,134,192]{1,2,0:T(8,128)(2,1)S(1)}, bf16[3,134,192]{1,2,0:T(8,128)(2,1)S(1)}, u32[]{:S(2)}, u32[]{:S(2)}) collective-permute-start(bf16[3,134,192]{1,2,0:T(8,128)(2,1)S(1)} %get-tuple-element.29), channel_id=1, source_target_pairs={{0,2},{2,4},{4,6},{6,8},{8,10},{10,12},{12,14},{1,3},{3,5},{5,7},{... | collective-permute-start | bytes 463112 | tf_op jit(solution)/shard_map/ppermute | solution.py:17
  60.9 1.5 collective-permute-start.7
  62.3 1.6 fusion.147
  63.9 0.6 multiply_cosine_fusion
  64.8 8.8 %collective-permute-done.6 = bf16[3,134,192]{1,2,0:T(8,128)(2,1)S(1)} collective-permute-done((bf16[3,134,192]{1,2,0:T(8,128)(2,1)S(1)}, bf16[3,134,192]{1,2,0:T(8,128)(2,1)S(1)}, u32[]{:S(2)}, u32[]{:S(2)}) %collective-permute-start.6) | collective-permute-done | bytes 154400 | tf_op jit(solution)/shard_map/ppermute | solution.py:17
  73.6 2.2 maximum_maximum_fusion.1
  76.3 18.0 %fusion.138 = (f32[16,128]{1,0:T(8,128)S(1)}, f32[16,128]{1,0:T(8,128)S(1)}, f32[16,128,192]{1,2,0:T(8,128)}) fusion(bf16[2,16,128,192]{2,3,1,0:T(8,128)(2,1)S(1)} %copy-done.6, bf16[19,134,192]{1,2,0:T(8,128)(2,1)S(1)} %get-tuple-element.28, f32[192]{0:T(256)S(1)} %bitcast.285, f32[192]{0:T(256)S(1)} %bitcast.287, f32[192]{0:T(256)S(1)} %bitcast.289, ...), kind=kLoop, calls=%fused_computation.192 | loop fusion | flops 66056192 | bytes 36266752 | tf_op jit(solution)/shard_map/reduce_sum | solution.py:50
  94.4 5.4 %multiply_add_fusion.1 = f32[16,128,192]{1,2,0:T(8,128)S(1)} fusion(f32[16,128,192]{1,2,0:T(8,128)} %get-tuple-element.150, bf16[2,16,128,768]{3,2,1,0:T(8,128)(2,1)} %param.17, f32[16,128,192]{1,2,0:T(8,128)} %get-tuple-element.17, f32[16,128]{1,0:T(8,128)S(1)} %broadcast_multiply_fusion.4, f32[16,128]{1,0:T(8,128)S(1)} %broadcast_multiply_fusion.5, ...), kind=kOutput, calls=%fused_computation.101 | convolution fusion | flops 1216217088 | bytes 9267200 | tf_op jit(solution)/shard_map/dot_general | solution.py:75
  99.9 6.0 %fusion.137 = (f32[16,128]{1,0:T(8,128)S(1)}, f32[16,128]{1,0:T(8,128)S(1)}, f32[16,128,192]{1,2,0:T(8,128)}) fusion(bf16[2,16,128,192]{2,3,1,0:T(8,128)(2,1)S(1)} %copy-done.7, bf16[2,192,768]{2,1,0:T(8,128)(2,1)} %param.12, bf16[2,16,128,768]{3,2,1,0:T(8,128)(2,1)} %param.17, f32[16,128,192]{1,2,0:T(8,128)S(1)} %multiply_add_fusion.1, ...), kind=kOutput, calls=%fused_computation.191 | convolution fusion | flops 1215819776 | bytes 7685696 | tf_op jit(solution)/shard_map/dot_general | solution.py:86
  105.9 1.7 fusion.49
  108.0 0.4 copy.27
  108.4 0.4 copy.28
  108.8 0.6 collective-permute-start.9
  109.6 0.4 copy.29
  110.2 0.4 copy.30
  110.7 0.4 pad_maximum_fusion.17
  111.0 1.3 collective-permute-start.10
  112.7 5.4 %collective-permute-start.11 = (bf16[3,134,192]{1,2,0:T(8,128)(2,1)S(1)}, bf16[3,134,192]{1,2,0:T(8,128)(2,1)S(1)}, u32[]{:S(2)}, u32[]{:S(2)}) collective-permute-start(bf16[3,134,192]{1,2,0:T(8,128)(2,1)S(1)} %get-tuple-element.26), channel_id=1, source_target_pairs={{0,2},{2,4},{4,6},{6,8},{8,10},{10,12},{12,14},{1,3},{3,5},{5,7},{... | collective-permute-start | bytes 463112 | tf_op jit(solution)/shard_map/ppermute | solution.py:17
  118.1 4.8 %collective-permute-done.10 = bf16[3,134,192]{1,2,0:T(8,128)(2,1)S(1)} collective-permute-done((bf16[3,134,192]{1,2,0:T(8,128)(2,1)S(1)}, bf16[3,134,192]{1,2,0:T(8,128)(2,1)S(1)}, u32[]{:S(2)}, u32[]{:S(2)}) %collective-permute-start.10) | collective-permute-done | bytes 154400 | tf_op jit(solution)/shard_map/ppermute | solution.py:18
  122.9 7.2 %collective-permute-done.11 = bf16[3,134,192]{1,2,0:T(8,128)(2,1)S(1)} collective-permute-done((bf16[3,134,192]{1,2,0:T(8,128)(2,1)S(1)}, bf16[3,134,192]{1,2,0:T(8,128)(2,1)S(1)}, u32[]{:S(2)}, u32[]{:S(2)}) %collective-permute-start.11) | collective-permute-done | bytes 154400 | tf_op jit(solution)/shard_map/ppermute | solution.py:17
  130.1 2.2 pad_maximum_fusion.2
  132.7 17.1 %multiply_add_fusion = f32[16,128,192]{1,2,0:T(8,128)} fusion(f32[16,128,192]{1,2,0:T(8,128)S(1)} %copy-done.1, bf16[16,128,192]{1,2,0:T(8,128)(2,1)S(1)} %fusion.49, bf16[16,3,192]{1,2,0:T(8,128)(2,1)S(1)} %copy.29, bf16[16,3,192]{1,2,0:T(8,128)(2,1)S(1)} %copy.30, bf16[19,134,192]{1,2,0:T(8,128)(2,1)S(1)} %get-tuple-element.24, ...), kind=kLoop, calls=%fused_computation.35 | loop fusion | flops 65273856 | bytes 37036864 | tf_op jit(solution)/shard_map/add | solution.py:94
  149.8 6.2 %fusion.136 = (f32[16,128]{1,0:T(8,128)S(1)}, f32[16,128]{1,0:T(8,128)S(1)}, f32[16,128,192]{1,2,0:T(8,128)}) fusion(bf16[2,16,128,192]{2,3,1,0:T(8,128)(2,1)} %param.15, bf16[2,192,768]{2,1,0:T(8,128)(2,1)} %param.12, bf16[2,16,128,768]{3,2,1,0:T(8,128)(2,1)} %param.17, f32[16,128,192]{1,2,0:T(8,128)} %multiply_add_fusion, f32[192]{0:T(256)} %bitcast, ...), kind=kOutput, calls=%fused_computation.190 | convolution fusion | flops 1215426560 | bytes 7686144 | tf_op jit(solution)/shard_map/dot_general | solution.py:86
  156.0 1.8 fusion.40
  158.1 0.4 copy.33
  158.6 0.4 copy.34
  158.9 0.5 collective-permute-start.13
  159.7 0.4 copy.35
  160.3 0.4 copy.36
  160.8 0.4 pad_maximum_fusion.14
  161.1 1.3 collective-permute-start.14
  162.4 5.3 %collective-permute-start.15 = (bf16[3,134,192]{1,2,0:T(8,128)(2,1)S(1)}, bf16[3,134,192]{1,2,0:T(8,128)(2,1)S(1)}, u32[]{:S(2)}, u32[]{:S(2)}) collective-permute-start(bf16[3,134,192]{1,2,0:T(8,128)(2,1)S(1)} %get-tuple-element.22), channel_id=1, source_target_pairs={{0,2},{2,4},{4,6},{6,8},{8,10},{10,12},{12,14},{1,3},{3,5},{5,7},{... | collective-permute-start | bytes 463112 | tf_op jit(solution)/shard_map/ppermute | solution.py:17
  167.7 0.7 cosine_reduce_fusion
  169.4 3.6 %collective-permute-done.14 = bf16[3,134,192]{1,2,0:T(8,128)(2,1)S(1)} collective-permute-done((bf16[3,134,192]{1,2,0:T(8,128)(2,1)S(1)}, bf16[3,134,192]{1,2,0:T(8,128)(2,1)S(1)}, u32[]{:S(2)}, u32[]{:S(2)}) %collective-permute-start.14) | collective-permute-done | bytes 154400 | tf_op jit(solution)/shard_map/ppermute | solution.py:18
  173.0 6.5 %collective-permute-done.15 = bf16[3,134,192]{1,2,0:T(8,128)(2,1)S(1)} collective-permute-done((bf16[3,134,192]{1,2,0:T(8,128)(2,1)S(1)}, bf16[3,134,192]{1,2,0:T(8,128)(2,1)S(1)}, u32[]{:S(2)}, u32[]{:S(2)}) %collective-permute-start.15) | collective-permute-done | bytes 154400 | tf_op jit(solution)/shard_map/ppermute | solution.py:17
  179.5 2.2 pad_maximum_fusion.3
  182.1 18.2 %fusion.31 = (f32[]{:T(128)}, f32[]{:T(128)}, f32[]{:T(128)}, f32[16,128,192]{1,2,0:T(8,128)}) fusion(f32[16,128,192]{1,2,0:T(8,128)S(1)} %copy-done.4, f32[16]{0:T(128)} %multiply_cosine_fusion, f32[16,128,192]{1,2,0:T(8,128)S(1)} %copy-done.2, f32[16,128,192]{1,2,0:T(8,128)S(1)} %copy-done.3, bf16[19,134,192]{1,2,0:T(8,128)(2,1)S(1)} %get-tuple-element.20, ...), kind=kLoop, calls=%fused_computation.80 | loop fusion | flops 68812800 | bytes 40182604 | tf_op jit(solution)/shard_map/reduce_sum | solution.py:77
  200.3 32.1 %all-reduce = (f32[]{:T(128)}, f32[]{:T(128)}, f32[]{:T(128)}) all-reduce(f32[]{:T(128)} %get-tuple-element.11, f32[]{:T(128)} %get-tuple-element.12, f32[]{:T(128)} %get-tuple-element.10), channel_id=1, replica_groups=mesh['grp'=2,'lat'=8,'lon'=2] {'lat','lon'}, use_global_device_ids=true, to_apply=%region_9.0 | all-reduce | flops 3 | bytes 24 | tf_op jit(solution)/shard_map/psum | solution.py:97
  234.4 2.8 %broadcast_divide_fusion = f32[16,128,192]{1,2,0:T(8,128)} fusion(f32[16,128,192]{1,2,0:T(8,128)} %get-tuple-element.16, f32[16]{0:T(128)S(1)} %broadcast_multiply_fusion.8), kind=kLoop, calls=%fused_computation.133 | loop fusion | flops 393216 | bytes 3145792 | tf_op jit(solution)/shard_map/div | solution.py:104
  (373 shorter events, 3.1 us)
Async XLA Ops:
  2.9 3.5 %collective-permute-start = (bf16[16,3,192]{2,0,1:T(8,128)(2,1)S(1)}, bf16[16,3,192]{2,0,1:T(8,128)(2,1)S(1)}, u32[]{:S(2)}, u32[]{:S(2)}) collective-permute-start(bf16[16,3,192]{2,0,1:T(8,128)(2,1)S(1)} %copy.14), channel_id=1, source_target_pairs={{0,1},{1,0},{2,3},{3,2},{4,5},{5,4},{6,7},{7,6},{8,9},{9,8},{10,11... | collective-permute-start | bytes 55304 | tf_op jit(solution)/shard_map/ppermute | solution.py:17
  3.8 3.0 %collective-permute-start.1 = (bf16[16,3,192]{2,0,1:T(8,128)(2,1)S(1)}, bf16[16,3,192]{2,0,1:T(8,128)(2,1)S(1)}, u32[]{:S(2)}, u32[]{:S(2)}) collective-permute-start(bf16[16,3,192]{2,0,1:T(8,128)(2,1)S(1)} %copy.15), channel_id=1, source_target_pairs={{1,0},{0,1},{3,2},{2,3},{5,4},{4,5},{7,6},{6,7},{9,8},{8,9},{11,10... | collective-permute-start | bytes 55304 | tf_op jit(solution)/shard_map/ppermute | solution.py:18
  4.1 50.5 %copy-start.9 = (f32[7,7,192]{2,1,0:T(8,128)}, f32[7,7,192]{2,1,0:T(8,128)S(1)}, u32[]{:S(2)}) copy-start(f32[7,7,192]{2,1,0:T(8,128)S(1)} %get-tuple-element.153) | copy-start | bytes 112900
  4.1 23.5 %copy-start.12 = (f32[1,1,192]{2,1,0:T(1,128)}, f32[1,1,192]{2,1,0:T(1,128)S(1)}, u32[]{:S(2)}) copy-start(f32[1,1,192]{2,1,0:T(1,128)S(1)} %get-tuple-element.113) | copy-start | bytes 2308
  4.1 23.5 %copy-start.14 = (f32[1,1,192]{2,1,0:T(1,128)}, f32[1,1,192]{2,1,0:T(1,128)S(1)}, u32[]{:S(2)}) copy-start(f32[1,1,192]{2,1,0:T(1,128)S(1)} %get-tuple-element.114) | copy-start | bytes 2308
  4.1 23.5 %copy-start.16 = (f32[1,1,192]{2,1,0:T(1,128)}, f32[1,1,192]{2,1,0:T(1,128)S(1)}, u32[]{:S(2)}) copy-start(f32[1,1,192]{2,1,0:T(1,128)S(1)} %get-tuple-element.115) | copy-start | bytes 2308
  4.1 23.5 %copy-start.18 = (f32[1,1,192]{2,1,0:T(1,128)}, f32[1,1,192]{2,1,0:T(1,128)S(1)}, u32[]{:S(2)}) copy-start(f32[1,1,192]{2,1,0:T(1,128)S(1)} %get-tuple-element.116) | copy-start | bytes 2308
  4.1 23.5 %copy-start.20 = (f32[1,1,192]{2,1,0:T(1,128)}, f32[1,1,192]{2,1,0:T(1,128)S(1)}, u32[]{:S(2)}) copy-start(f32[1,1,192]{2,1,0:T(1,128)S(1)} %get-tuple-element.117) | copy-start | bytes 2308
  4.1 23.5 %copy-start.22 = (f32[1,1,192]{2,1,0:T(1,128)}, f32[1,1,192]{2,1,0:T(1,128)S(1)}, u32[]{:S(2)}) copy-start(f32[1,1,192]{2,1,0:T(1,128)S(1)} %get-tuple-element.118) | copy-start | bytes 2308
  4.1 23.5 %copy-start.24 = (f32[1,1,192]{2,1,0:T(1,128)}, f32[1,1,192]{2,1,0:T(1,128)S(1)}, u32[]{:S(2)}) copy-start(f32[1,1,192]{2,1,0:T(1,128)S(1)} %get-tuple-element.119) | copy-start | bytes 2308
  4.2 23.5 %copy-start.26 = (f32[1,1,192]{2,1,0:T(1,128)}, f32[1,1,192]{2,1,0:T(1,128)S(1)}, u32[]{:S(2)}) copy-start(f32[1,1,192]{2,1,0:T(1,128)S(1)} %get-tuple-element.120) | copy-start | bytes 2308
  4.2 23.5 %copy-start.28 = (f32[1,1,192]{2,1,0:T(1,128)}, f32[1,1,192]{2,1,0:T(1,128)S(1)}, u32[]{:S(2)}) copy-start(f32[1,1,192]{2,1,0:T(1,128)S(1)} %get-tuple-element.121) | copy-start | bytes 2308
  4.2 23.5 %copy-start.30 = (f32[1,1,192]{2,1,0:T(1,128)}, f32[1,1,192]{2,1,0:T(1,128)S(1)}, u32[]{:S(2)}) copy-start(f32[1,1,192]{2,1,0:T(1,128)S(1)} %get-tuple-element.122) | copy-start | bytes 2308
  4.2 23.5 %copy-start.32 = (f32[1,1,192]{2,1,0:T(1,128)}, f32[1,1,192]{2,1,0:T(1,128)S(1)}, u32[]{:S(2)}) copy-start(f32[1,1,192]{2,1,0:T(1,128)S(1)} %get-tuple-element.123) | copy-start | bytes 2308
  4.2 23.5 %copy-start.34 = (f32[1,1,192]{2,1,0:T(1,128)}, f32[1,1,192]{2,1,0:T(1,128)S(1)}, u32[]{:S(2)}) copy-start(f32[1,1,192]{2,1,0:T(1,128)S(1)} %get-tuple-element.124) | copy-start | bytes 2308
  4.2 23.5 %copy-start.36 = (f32[1,1,192]{2,1,0:T(1,128)}, f32[1,1,192]{2,1,0:T(1,128)S(1)}, u32[]{:S(2)}) copy-start(f32[1,1,192]{2,1,0:T(1,128)S(1)} %get-tuple-element.125) | copy-start | bytes 2308
  4.2 23.5 %copy-start.38 = (f32[1,1,192]{2,1,0:T(1,128)}, f32[1,1,192]{2,1,0:T(1,128)S(1)}, u32[]{:S(2)}) copy-start(f32[1,1,192]{2,1,0:T(1,128)S(1)} %get-tuple-element.126) | copy-start | bytes 2308
  4.2 23.5 %copy-start.40 = (f32[1,1,192]{2,1,0:T(1,128)}, f32[1,1,192]{2,1,0:T(1,128)S(1)}, u32[]{:S(2)}) copy-start(f32[1,1,192]{2,1,0:T(1,128)S(1)} %get-tuple-element.127) | copy-start | bytes 2308
  4.2 23.5 %copy-start.42 = (f32[1,1,192]{2,1,0:T(1,128)}, f32[1,1,192]{2,1,0:T(1,128)S(1)}, u32[]{:S(2)}) copy-start(f32[1,1,192]{2,1,0:T(1,128)S(1)} %get-tuple-element.128) | copy-start | bytes 2308
  4.2 23.5 %copy-start.44 = (f32[1,1,192]{2,1,0:T(1,128)}, f32[1,1,192]{2,1,0:T(1,128)S(1)}, u32[]{:S(2)}) copy-start(f32[1,1,192]{2,1,0:T(1,128)S(1)} %get-tuple-element.129) | copy-start | bytes 2308
  4.3 23.5 %copy-start.46 = (f32[1,1,192]{2,1,0:T(1,128)}, f32[1,1,192]{2,1,0:T(1,128)S(1)}, u32[]{:S(2)}) copy-start(f32[1,1,192]{2,1,0:T(1,128)S(1)} %get-tuple-element.130) | copy-start | bytes 2308
  4.3 23.5 %copy-start.48 = (f32[1,1,192]{2,1,0:T(1,128)}, f32[1,1,192]{2,1,0:T(1,128)S(1)}, u32[]{:S(2)}) copy-start(f32[1,1,192]{2,1,0:T(1,128)S(1)} %get-tuple-element.131) | copy-start | bytes 2308
  4.3 23.4 %copy-start.50 = (f32[1,1,192]{2,1,0:T(1,128)}, f32[1,1,192]{2,1,0:T(1,128)S(1)}, u32[]{:S(2)}) copy-start(f32[1,1,192]{2,1,0:T(1,128)S(1)} %get-tuple-element.94) | copy-start | bytes 2308
  4.3 23.4 %copy-start.52 = (f32[1,1,192]{2,1,0:T(1,128)}, f32[1,1,192]{2,1,0:T(1,128)S(1)}, u32[]{:S(2)}) copy-start(f32[1,1,192]{2,1,0:T(1,128)S(1)} %get-tuple-element.95) | copy-start | bytes 2308
  4.3 23.4 %copy-start.54 = (f32[1,1,192]{2,1,0:T(1,128)}, f32[1,1,192]{2,1,0:T(1,128)S(1)}, u32[]{:S(2)}) copy-start(f32[1,1,192]{2,1,0:T(1,128)S(1)} %get-tuple-element.96) | copy-start | bytes 2308
  4.3 23.4 %copy-start.56 = (f32[1,1,192]{2,1,0:T(1,128)}, f32[1,1,192]{2,1,0:T(1,128)S(1)}, u32[]{:S(2)}) copy-start(f32[1,1,192]{2,1,0:T(1,128)S(1)} %get-tuple-element.97) | copy-start | bytes 2308
  4.3 23.4 %copy-start.58 = (f32[1,1,192]{2,1,0:T(1,128)}, f32[1,1,192]{2,1,0:T(1,128)S(1)}, u32[]{:S(2)}) copy-start(f32[1,1,192]{2,1,0:T(1,128)S(1)} %get-tuple-element.98) | copy-start | bytes 2308
  4.4 23.4 %copy-start.60 = (f32[1,1,192]{2,1,0:T(1,128)}, f32[1,1,192]{2,1,0:T(1,128)S(1)}, u32[]{:S(2)}) copy-start(f32[1,1,192]{2,1,0:T(1,128)S(1)} %get-tuple-element.99) | copy-start | bytes 2308
  4.4 23.4 %copy-start.62 = (f32[1,1,192]{2,1,0:T(1,128)}, f32[1,1,192]{2,1,0:T(1,128)S(1)}, u32[]{:S(2)}) copy-start(f32[1,1,192]{2,1,0:T(1,128)S(1)} %get-tuple-element.100) | copy-start | bytes 2308
  4.4 23.4 %copy-start.64 = (f32[1,1,192]{2,1,0:T(1,128)}, f32[1,1,192]{2,1,0:T(1,128)S(1)}, u32[]{:S(2)}) copy-start(f32[1,1,192]{2,1,0:T(1,128)S(1)} %get-tuple-element.101) | copy-start | bytes 2308
  4.4 23.4 %copy-start.66 = (f32[1,1,192]{2,1,0:T(1,128)}, f32[1,1,192]{2,1,0:T(1,128)S(1)}, u32[]{:S(2)}) copy-start(f32[1,1,192]{2,1,0:T(1,128)S(1)} %get-tuple-element.102) | copy-start | bytes 2308
  4.4 23.4 %copy-start.68 = (f32[1,1,192]{2,1,0:T(1,128)}, f32[1,1,192]{2,1,0:T(1,128)S(1)}, u32[]{:S(2)}) copy-start(f32[1,1,192]{2,1,0:T(1,128)S(1)} %get-tuple-element.103) | copy-start | bytes 2308
  4.4 23.4 %copy-start.70 = (f32[1,1,192]{2,1,0:T(1,128)}, f32[1,1,192]{2,1,0:T(1,128)S(1)}, u32[]{:S(2)}) copy-start(f32[1,1,192]{2,1,0:T(1,128)S(1)} %get-tuple-element.104) | copy-start | bytes 2308
  4.4 23.4 %copy-start.72 = (f32[1,1,192]{2,1,0:T(1,128)}, f32[1,1,192]{2,1,0:T(1,128)S(1)}, u32[]{:S(2)}) copy-start(f32[1,1,192]{2,1,0:T(1,128)S(1)} %get-tuple-element.105) | copy-start | bytes 2308
  4.4 23.4 %copy-start.74 = (f32[1,1,192]{2,1,0:T(1,128)}, f32[1,1,192]{2,1,0:T(1,128)S(1)}, u32[]{:S(2)}) copy-start(f32[1,1,192]{2,1,0:T(1,128)S(1)} %get-tuple-element.106) | copy-start | bytes 2308
  4.4 23.4 %copy-start.76 = (f32[1,1,192]{2,1,0:T(1,128)}, f32[1,1,192]{2,1,0:T(1,128)S(1)}, u32[]{:S(2)}) copy-start(f32[1,1,192]{2,1,0:T(1,128)S(1)} %get-tuple-element.107) | copy-start | bytes 2308
  4.4 23.4 %copy-start.78 = (f32[1,1,192]{2,1,0:T(1,128)}, f32[1,1,192]{2,1,0:T(1,128)S(1)}, u32[]{:S(2)}) copy-start(f32[1,1,192]{2,1,0:T(1,128)S(1)} %get-tuple-element.108) | copy-start | bytes 2308
  4.5 23.4 %copy-start.80 = (f32[1,1,192]{2,1,0:T(1,128)}, f32[1,1,192]{2,1,0:T(1,128)S(1)}, u32[]{:S(2)}) copy-start(f32[1,1,192]{2,1,0:T(1,128)S(1)} %get-tuple-element.109) | copy-start | bytes 2308
  4.5 23.4 %copy-start.82 = (f32[1,1,192]{2,1,0:T(1,128)}, f32[1,1,192]{2,1,0:T(1,128)S(1)}, u32[]{:S(2)}) copy-start(f32[1,1,192]{2,1,0:T(1,128)S(1)} %get-tuple-element.110) | copy-start | bytes 2308
  4.5 23.4 %copy-start.84 = (f32[1,1,192]{2,1,0:T(1,128)}, f32[1,1,192]{2,1,0:T(1,128)S(1)}, u32[]{:S(2)}) copy-start(f32[1,1,192]{2,1,0:T(1,128)S(1)} %get-tuple-element.111) | copy-start | bytes 2308
  4.5 23.4 %copy-start.86 = (f32[1,1,192]{2,1,0:T(1,128)}, f32[1,1,192]{2,1,0:T(1,128)S(1)}, u32[]{:S(2)}) copy-start(f32[1,1,192]{2,1,0:T(1,128)S(1)} %get-tuple-element.112) | copy-start | bytes 2308
  7.7 17.6 %collective-permute-start.2 = (bf16[3,134,192]{1,2,0:T(8,128)(2,1)S(1)}, bf16[3,134,192]{1,2,0:T(8,128)(2,1)S(1)}, u32[]{:S(2)}, u32[]{:S(2)}) collective-permute-start(bf16[3,134,192]{1,2,0:T(8,128)(2,1)S(1)} %get-tuple-element.33), channel_id=1, source_target_pairs={{0,2},{2,4},{4,6},{6,8},{8,10},{10,12},{12,14},{1,3},{3,5},{5,7},{... | collective-permute-start | bytes 463112 | tf_op jit(solution)/shard_map/ppermute | solution.py:17
  12.6 12.7 %collective-permute-start.3 = (bf16[3,134,192]{1,2,0:T(8,128)(2,1)S(1)}, bf16[3,134,192]{1,2,0:T(8,128)(2,1)S(1)}, u32[]{:S(2)}, u32[]{:S(2)}) collective-permute-start(bf16[3,134,192]{1,2,0:T(8,128)(2,1)S(1)} %get-tuple-element.34), channel_id=1, source_target_pairs={{2,0},{4,2},{6,4},{8,6},{10,8},{12,10},{14,12},{3,1},{5,3},{7,5},{... | collective-permute-start | bytes 463112 | tf_op jit(solution)/shard_map/ppermute | solution.py:18
  53.5 1.7 collective-permute-start.4
  54.0 1.7 collective-permute-start.5
  56.4 17.2 %collective-permute-start.6 = (bf16[3,134,192]{1,2,0:T(8,128)(2,1)S(1)}, bf16[3,134,192]{1,2,0:T(8,128)(2,1)S(1)}, u32[]{:S(2)}, u32[]{:S(2)}) collective-permute-start(bf16[3,134,192]{1,2,0:T(8,128)(2,1)S(1)} %get-tuple-element.29), channel_id=1, source_target_pairs={{0,2},{2,4},{4,6},{6,8},{8,10},{10,12},{12,14},{1,3},{3,5},{5,7},{... | collective-permute-start | bytes 463112 | tf_op jit(solution)/shard_map/ppermute | solution.py:17
  60.9 12.8 %collective-permute-start.7 = (bf16[3,134,192]{1,2,0:T(8,128)(2,1)S(1)}, bf16[3,134,192]{1,2,0:T(8,128)(2,1)S(1)}, u32[]{:S(2)}, u32[]{:S(2)}) collective-permute-start(bf16[3,134,192]{1,2,0:T(8,128)(2,1)S(1)} %get-tuple-element.30), channel_id=1, source_target_pairs={{2,0},{4,2},{6,4},{8,6},{10,8},{12,10},{14,12},{3,1},{5,3},{7,5},{... | collective-permute-start | bytes 463112 | tf_op jit(solution)/shard_map/ppermute | solution.py:18
  108.4 1.3 collective-permute-start.8
  108.8 1.4 collective-permute-start.9
  111.0 11.9 %collective-permute-start.10 = (bf16[3,134,192]{1,2,0:T(8,128)(2,1)S(1)}, bf16[3,134,192]{1,2,0:T(8,128)(2,1)S(1)}, u32[]{:S(2)}, u32[]{:S(2)}) collective-permute-start(bf16[3,134,192]{1,2,0:T(8,128)(2,1)S(1)} %get-tuple-element.25), channel_id=1, source_target_pairs={{2,0},{4,2},{6,4},{8,6},{10,8},{12,10},{14,12},{3,1},{5,3},{7,5},{... | collective-permute-start | bytes 463112 | tf_op jit(solution)/shard_map/ppermute | solution.py:18
  112.3 20.0 %copy-start.1 = (f32[16,128,192]{1,2,0:T(8,128)S(1)}, f32[16,128,192]{1,2,0:T(8,128)}, u32[]{:S(2)}) copy-start(f32[16,128,192]{1,2,0:T(8,128)} %copy-done) | copy-start | bytes 4718596
  112.3 20.0 %copy-start.88 = (f32[1,1,192]{2,1,0:T(1,128)S(1)}, f32[1,1,192]{2,1,0:T(1,128)}, u32[]{:S(2)}) copy-start(f32[1,1,192]{2,1,0:T(1,128)} %get-tuple-element.45) | copy-start | bytes 2308
  112.3 20.0 %copy-start.90 = (f32[1,1,192]{2,1,0:T(1,128)S(1)}, f32[1,1,192]{2,1,0:T(1,128)}, u32[]{:S(2)}) copy-start(f32[1,1,192]{2,1,0:T(1,128)} %get-tuple-element.46) | copy-start | bytes 2308
  112.4 20.0 %copy-start.92 = (f32[1,1,192]{2,1,0:T(1,128)S(1)}, f32[1,1,192]{2,1,0:T(1,128)}, u32[]{:S(2)}) copy-start(f32[1,1,192]{2,1,0:T(1,128)} %get-tuple-element.47) | copy-start | bytes 2308
  112.4 20.0 %copy-start.94 = (f32[1,1,192]{2,1,0:T(1,128)S(1)}, f32[1,1,192]{2,1,0:T(1,128)}, u32[]{:S(2)}) copy-start(f32[1,1,192]{2,1,0:T(1,128)} %get-tuple-element.48) | copy-start | bytes 2308
  112.4 20.0 %copy-start.96 = (f32[1,1,192]{2,1,0:T(1,128)S(1)}, f32[1,1,192]{2,1,0:T(1,128)}, u32[]{:S(2)}) copy-start(f32[1,1,192]{2,1,0:T(1,128)} %get-tuple-element.49) | copy-start | bytes 2308
  112.4 20.0 %copy-start.98 = (f32[1,1,192]{2,1,0:T(1,128)S(1)}, f32[1,1,192]{2,1,0:T(1,128)}, u32[]{:S(2)}) copy-start(f32[1,1,192]{2,1,0:T(1,128)} %get-tuple-element.50) | copy-start | bytes 2308
  112.4 20.0 %copy-start.100 = (f32[1,1,192]{2,1,0:T(1,128)S(1)}, f32[1,1,192]{2,1,0:T(1,128)}, u32[]{:S(2)}) copy-start(f32[1,1,192]{2,1,0:T(1,128)} %get-tuple-element.51) | copy-start | bytes 2308
  112.4 20.0 %copy-start.102 = (f32[1,1,192]{2,1,0:T(1,128)S(1)}, f32[1,1,192]{2,1,0:T(1,128)}, u32[]{:S(2)}) copy-start(f32[1,1,192]{2,1,0:T(1,128)} %get-tuple-element.52) | copy-start | bytes 2308
  112.7 17.4 %collective-permute-start.11 = (bf16[3,134,192]{1,2,0:T(8,128)(2,1)S(1)}, bf16[3,134,192]{1,2,0:T(8,128)(2,1)S(1)}, u32[]{:S(2)}, u32[]{:S(2)}) collective-permute-start(bf16[3,134,192]{1,2,0:T(8,128)(2,1)S(1)} %get-tuple-element.26), channel_id=1, source_target_pairs={{0,2},{2,4},{4,6},{6,8},{8,10},{10,12},{12,14},{1,3},{3,5},{5,7},{... | collective-permute-start | bytes 463112 | tf_op jit(solution)/shard_map/ppermute | solution.py:17
  158.5 1.3 collective-permute-start.12
  158.9 1.4 collective-permute-start.13
  161.1 11.9 %collective-permute-start.14 = (bf16[3,134,192]{1,2,0:T(8,128)(2,1)S(1)}, bf16[3,134,192]{1,2,0:T(8,128)(2,1)S(1)}, u32[]{:S(2)}, u32[]{:S(2)}) collective-permute-start(bf16[3,134,192]{1,2,0:T(8,128)(2,1)S(1)} %get-tuple-element.21), channel_id=1, source_target_pairs={{2,0},{4,2},{6,4},{8,6},{10,8},{12,10},{14,12},{3,1},{5,3},{7,5},{... | collective-permute-start | bytes 463112 | tf_op jit(solution)/shard_map/ppermute | solution.py:18
  162.4 17.1 %collective-permute-start.15 = (bf16[3,134,192]{1,2,0:T(8,128)(2,1)S(1)}, bf16[3,134,192]{1,2,0:T(8,128)(2,1)S(1)}, u32[]{:S(2)}, u32[]{:S(2)}) collective-permute-start(bf16[3,134,192]{1,2,0:T(8,128)(2,1)S(1)} %get-tuple-element.22), channel_id=1, source_target_pairs={{0,2},{2,4},{4,6},{6,8},{8,10},{10,12},{12,14},{1,3},{3,5},{5,7},{... | collective-permute-start | bytes 463112 | tf_op jit(solution)/shard_map/ppermute | solution.py:17
  (123 other events, 1667.6 us)
where the time goes:
time: 239 us; the launch traced here: 238 us
  other arithmetic  91.1 us (38%)
  waiting for transfers between devices  42.6 us (18%)
  blocking collectives  32.1 us (13%)
  starting transfers between devices  27.8 us (12%)
  matrix products  24.1 us (10%)
  local copies, waits for them, and re-layouts  13.4 us (6%)
  between operations  7.26 us (3%)
    reduce_sum x2, other arithmetic, project(): jnp.mean(values, axis=-1, keepdims=True)  36.4 us
    ppermute x8, waiting for transfers between devices, extended(): before = lax.ppermute(last, axis, up)  33.8 us
    psum x1, blocking collectives, on_device(): lax.psum((start_local, forward_local, adjoint_local), ('lat', 'lon'))  32.1 us
    ppermute x8, starting transfers between devices, extended(): before = lax.ppermute(last, axis, up)  20.7 us
    reduce_sum x1, other arithmetic, on_device(): start_local = jnp.sum(area_w * perturb * perturb)  18.2 us
    add x1, other arithmetic, on_device(): grad_field = grad_field + conv_back  17.1 us
    dot_general x2, matrix products, on_device(): lax.dot_general(gated, w_in[layer_index], (((2,), (1,)), ((), ())), prefe...  12.2 us
    dot_general x2, matrix products, on_device(): jnp.dot(gated, w_out[layer_index], preferred_element_type=jnp.float32)  11.9 us
  transfers between devices with their start and end apart: 16, of which 10 were waited for; matrix products, arithmetic and copies ran while one was open for 4% of the time, Pallas kernels for 0%

commit v1 on v0

--- a/solution.py
+++ b/solution.py
@@ -95,7 +95,7 @@
     adjoint_out = grad_field / area_w
     adjoint_local = jnp.sum(area_w * adjoint_out * adjoint_out)
     start_sum, forward_sum, adjoint_sum = lax.psum(
-        (start_local, forward_local, adjoint_local), ("lat", "lon")
+        lax.psum((start_local, forward_local, adjoint_local), "lon"), "lat"
     )
     start_sq = start_sum / weight_total
     forward_sq = forward_sum / weight_total

time: 239 us -> 231 us (0.967)
  blocking collectives: 32.1 us -> 23.8 us
    psum x1 -> x2, blocking collectives: 32.1 us -> 23.8 us  [the longest x1 20.6 us: on_device(): lax.psum(lax.psum((start_local, forward_local, adjoint_local), 'lon'), 'l...]
where the time goes in v1:
time: 231 us; the launch traced here: 230 us
  other arithmetic  91.2 us (39%)
  waiting for transfers between devices  42.4 us (18%)
  starting transfers between devices  27.8 us (12%)
  matrix products  24.1 us (10%)
  blocking collectives  23.8 us (10%)
  local copies, waits for them, and re-layouts  13.4 us (6%)
  between operations  7.33 us (3%)
    reduce_sum x2, other arithmetic, project(): jnp.mean(values, axis=-1, keepdims=True)  36.3 us
    ppermute x8, waiting for transfers between devices, extended(): before = lax.ppermute(last, axis, up)  33.8 us
    ppermute x8, starting transfers between devices, extended(): before = lax.ppermute(last, axis, up)  20.7 us
    psum x1, blocking collectives, on_device(): lax.psum(lax.psum((start_local, forward_local, adjoint_local), 'lon'), 'l...  20.6 us
    reduce_sum x1, other arithmetic, on_device(): start_local = jnp.sum(area_w * perturb * perturb)  18.2 us
    add x1, other arithmetic, on_device(): grad_field = grad_field + conv_back  17.1 us
    dot_general x2, matrix products, on_device(): lax.dot_general(gated, w_in[layer_index], (((2,), (1,)), ((), ())), prefe...  12.2 us
    dot_general x2, matrix products, on_device(): jnp.dot(gated, w_out[layer_index], preferred_element_type=jnp.float32)  11.9 us
  transfers between devices with their start and end apart: 16, of which 10 were waited for; matrix products, arithmetic and copies ran while one was open for 4% of the time, Pallas kernels for 0%

profile of v1, /device:TPU:0, one launch (start us, length us, event | category | flops | bytes accessed | tf_op | source)
XLA Modules:
  0.0 230.0 jit_solution(1334064928215537087)
XLA Ops:
  0.6 1.5 convert_element_type.665
  2.5 0.4 copy.14
  2.9 0.5 collective-permute-start
  3.4 0.4 copy.15
  4.5 0.6 fusion.150
  5.1 0.7 fusion.145
  5.8 0.6 fusion.151
  6.4 0.4 copy.16
  6.9 0.4 copy.17
  7.3 0.4 pad_maximum_fusion.23
  7.7 4.9 %collective-permute-start.2 = (bf16[3,134,192]{1,2,0:T(8,128)(2,1)S(1)}, bf16[3,134,192]{1,2,0:T(8,128)(2,1)S(1)}, u32[]{:S(2)}, u32[]{:S(2)}) collective-permute-start(bf16[3,134,192]{1,2,0:T(8,128)(2,1)S(1)} %get-tuple-element.36), channel_id=1, source_target_pairs={{0,2},{2,4},{4,6},{6,8},{8,10},{10,12},{12,14},{1,3},{3,5},{5,7},{... | collective-permute-start | bytes 463112 | tf_op jit(solution)/shard_map/ppermute | solution.py:17
  12.6 1.3 collective-permute-start.3
  13.9 0.6 fusion.152
  14.5 10.8 %collective-permute-done.2 = bf16[3,134,192]{1,2,0:T(8,128)(2,1)S(1)} collective-permute-done((bf16[3,134,192]{1,2,0:T(8,128)(2,1)S(1)}, bf16[3,134,192]{1,2,0:T(8,128)(2,1)S(1)}, u32[]{:S(2)}, u32[]{:S(2)}) %collective-permute-start.2) | collective-permute-done | bytes 154400 | tf_op jit(solution)/shard_map/ppermute | solution.py:17
  25.3 2.2 maximum_maximum_fusion
  28.0 18.3 %fusion.139 = (f32[16,128]{1,0:T(8,128)S(1)}, f32[16,128]{1,0:T(8,128)S(1)}, f32[16,128,192]{1,2,0:T(8,128)}) fusion(bf16[2,16,128,192]{2,3,1,0:T(8,128)(2,1)S(1)} %copy-done.5, bf16[19,134,192]{1,2,0:T(8,128)(2,1)S(1)} %get-tuple-element.35, f32[192]{0:T(256)S(1)} %bitcast.247, f32[192]{0:T(256)S(1)} %bitcast.249, f32[192]{0:T(256)S(1)} %bitcast.251, ...), kind=kLoop, calls=%fused_computation.193 | loop fusion | flops 66056192 | bytes 36266752 | tf_op jit(solution)/shard_map/reduce_sum | solution.py:50
  46.3 6.5 %fusion.153 = (bf16[16,128,192]{1,2,0:T(8,128)(2,1)S(1)}, f32[16,128,192]{1,2,0:T(8,128)}) fusion(f32[16,128,192]{1,2,0:T(8,128)} %param.9, bf16[2,768,192]{1,2,0:T(8,128)(2,1)S(1)} %copy-done.170, bf16[2,16,128,768]{3,2,1,0:T(8,128)(2,1)} %param.17, f32[16,128,192]{1,2,0:T(8,128)} %get-tuple-element.21, f32[16,128]{1,0:T(8,128)S(1)} %broadcast_multiply_fusion.6, ...), kind=kOutput, calls=%fused_computation.207 | convolution fusion | flops 1216610304 | bytes 10053632 | tf_op jit(solution)/shard_map/dot_general | solution.py:75
  53.1 0.4 copy.21
  53.6 0.4 copy.22
  54.0 0.6 collective-permute-start.5
  54.5 0.7 fusion.146
  55.2 0.4 copy.23
  55.6 0.4 copy.24
  56.1 0.4 pad_maximum_fusion.20
  56.4 4.4 %collective-permute-start.6 = (bf16[3,134,192]{1,2,0:T(8,128)(2,1)S(1)}, bf16[3,134,192]{1,2,0:T(8,128)(2,1)S(1)}, u32[]{:S(2)}, u32[]{:S(2)}) collective-permute-start(bf16[3,134,192]{1,2,0:T(8,128)(2,1)S(1)} %get-tuple-element.32), channel_id=1, source_target_pairs={{0,2},{2,4},{4,6},{6,8},{8,10},{10,12},{12,14},{1,3},{3,5},{5,7},{... | collective-permute-start | bytes 463112 | tf_op jit(solution)/shard_map/ppermute | solution.py:17
  60.9 1.5 collective-permute-start.7
  62.3 1.6 fusion.147
  63.9 0.6 multiply_cosine_fusion
  64.8 8.8 %collective-permute-done.6 = bf16[3,134,192]{1,2,0:T(8,128)(2,1)S(1)} collective-permute-done((bf16[3,134,192]{1,2,0:T(8,128)(2,1)S(1)}, bf16[3,134,192]{1,2,0:T(8,128)(2,1)S(1)}, u32[]{:S(2)}, u32[]{:S(2)}) %collective-permute-start.6) | collective-permute-done | bytes 154400 | tf_op jit(solution)/shard_map/ppermute | solution.py:17
  73.7 2.2 maximum_maximum_fusion.1
  76.3 18.0 %fusion.138 = (f32[16,128]{1,0:T(8,128)S(1)}, f32[16,128]{1,0:T(8,128)S(1)}, f32[16,128,192]{1,2,0:T(8,128)}) fusion(bf16[2,16,128,192]{2,3,1,0:T(8,128)(2,1)S(1)} %copy-done.6, bf16[19,134,192]{1,2,0:T(8,128)(2,1)S(1)} %get-tuple-element.31, f32[192]{0:T(256)S(1)} %bitcast.285, f32[192]{0:T(256)S(1)} %bitcast.287, f32[192]{0:T(256)S(1)} %bitcast.289, ...), kind=kLoop, calls=%fused_computation.192 | loop fusion | flops 66056192 | bytes 36266752 | tf_op jit(solution)/shard_map/reduce_sum | solution.py:50
  94.4 5.4 %multiply_add_fusion.1 = f32[16,128,192]{1,2,0:T(8,128)S(1)} fusion(f32[16,128,192]{1,2,0:T(8,128)} %get-tuple-element.153, bf16[2,16,128,768]{3,2,1,0:T(8,128)(2,1)} %param.17, f32[16,128,192]{1,2,0:T(8,128)} %get-tuple-element.20, f32[16,128]{1,0:T(8,128)S(1)} %broadcast_multiply_fusion.4, f32[16,128]{1,0:T(8,128)S(1)} %broadcast_multiply_fusion.5, ...), kind=kOutput, calls=%fused_computation.101 | convolution fusion | flops 1216217088 | bytes 9267200 | tf_op jit(solution)/shard_map/dot_general | solution.py:75
  99.9 6.0 %fusion.137 = (f32[16,128]{1,0:T(8,128)S(1)}, f32[16,128]{1,0:T(8,128)S(1)}, f32[16,128,192]{1,2,0:T(8,128)}) fusion(bf16[2,16,128,192]{2,3,1,0:T(8,128)(2,1)S(1)} %copy-done.7, bf16[2,192,768]{2,1,0:T(8,128)(2,1)} %param.12, bf16[2,16,128,768]{3,2,1,0:T(8,128)(2,1)} %param.17, f32[16,128,192]{1,2,0:T(8,128)S(1)} %multiply_add_fusion.1, ...), kind=kOutput, calls=%fused_computation.191 | convolution fusion | flops 1215819776 | bytes 7685696 | tf_op jit(solution)/shard_map/dot_general | solution.py:86
  105.9 1.7 fusion.49
  108.0 0.4 copy.27
  108.4 0.4 copy.28
  108.8 0.6 collective-permute-start.9
  109.6 0.4 copy.29
  110.2 0.4 copy.30
  110.7 0.4 pad_maximum_fusion.17
  111.0 1.3 collective-permute-start.10
  112.7 5.4 %collective-permute-start.11 = (bf16[3,134,192]{1,2,0:T(8,128)(2,1)S(1)}, bf16[3,134,192]{1,2,0:T(8,128)(2,1)S(1)}, u32[]{:S(2)}, u32[]{:S(2)}) collective-permute-start(bf16[3,134,192]{1,2,0:T(8,128)(2,1)S(1)} %get-tuple-element.29), channel_id=1, source_target_pairs={{0,2},{2,4},{4,6},{6,8},{8,10},{10,12},{12,14},{1,3},{3,5},{5,7},{... | collective-permute-start | bytes 463112 | tf_op jit(solution)/shard_map/ppermute | solution.py:17
  118.1 4.8 %collective-permute-done.10 = bf16[3,134,192]{1,2,0:T(8,128)(2,1)S(1)} collective-permute-done((bf16[3,134,192]{1,2,0:T(8,128)(2,1)S(1)}, bf16[3,134,192]{1,2,0:T(8,128)(2,1)S(1)}, u32[]{:S(2)}, u32[]{:S(2)}) %collective-permute-start.10) | collective-permute-done | bytes 154400 | tf_op jit(solution)/shard_map/ppermute | solution.py:18
  122.9 7.2 %collective-permute-done.11 = bf16[3,134,192]{1,2,0:T(8,128)(2,1)S(1)} collective-permute-done((bf16[3,134,192]{1,2,0:T(8,128)(2,1)S(1)}, bf16[3,134,192]{1,2,0:T(8,128)(2,1)S(1)}, u32[]{:S(2)}, u32[]{:S(2)}) %collective-permute-start.11) | collective-permute-done | bytes 154400 | tf_op jit(solution)/shard_map/ppermute | solution.py:17
  130.1 2.2 pad_maximum_fusion.2
  132.7 17.1 %multiply_add_fusion = f32[16,128,192]{1,2,0:T(8,128)} fusion(f32[16,128,192]{1,2,0:T(8,128)S(1)} %copy-done.1, bf16[16,128,192]{1,2,0:T(8,128)(2,1)S(1)} %fusion.49, bf16[16,3,192]{1,2,0:T(8,128)(2,1)S(1)} %copy.29, bf16[16,3,192]{1,2,0:T(8,128)(2,1)S(1)} %copy.30, bf16[19,134,192]{1,2,0:T(8,128)(2,1)S(1)} %get-tuple-element.27, ...), kind=kLoop, calls=%fused_computation.35 | loop fusion | flops 65273856 | bytes 37036864 | tf_op jit(solution)/shard_map/add | solution.py:94
  149.8 6.2 %fusion.136 = (f32[16,128]{1,0:T(8,128)S(1)}, f32[16,128]{1,0:T(8,128)S(1)}, f32[16,128,192]{1,2,0:T(8,128)}) fusion(bf16[2,16,128,192]{2,3,1,0:T(8,128)(2,1)} %param.15, bf16[2,192,768]{2,1,0:T(8,128)(2,1)} %param.12, bf16[2,16,128,768]{3,2,1,0:T(8,128)(2,1)} %param.17, f32[16,128,192]{1,2,0:T(8,128)} %multiply_add_fusion, f32[192]{0:T(256)} %bitcast, ...), kind=kOutput, calls=%fused_computation.190 | convolution fusion | flops 1215426560 | bytes 7686144 | tf_op jit(solution)/shard_map/dot_general | solution.py:86
  156.0 1.8 fusion.40
  158.1 0.4 copy.33
  158.6 0.4 copy.34
  158.9 0.5 collective-permute-start.13
  159.7 0.4 copy.35
  160.3 0.4 copy.36
  160.8 0.4 pad_maximum_fusion.14
  161.1 1.3 collective-permute-start.14
  162.4 5.3 %collective-permute-start.15 = (bf16[3,134,192]{1,2,0:T(8,128)(2,1)S(1)}, bf16[3,134,192]{1,2,0:T(8,128)(2,1)S(1)}, u32[]{:S(2)}, u32[]{:S(2)}) collective-permute-start(bf16[3,134,192]{1,2,0:T(8,128)(2,1)S(1)} %get-tuple-element.25), channel_id=1, source_target_pairs={{0,2},{2,4},{4,6},{6,8},{8,10},{10,12},{12,14},{1,3},{3,5},{5,7},{... | collective-permute-start | bytes 463112 | tf_op jit(solution)/shard_map/ppermute | solution.py:17
  167.7 0.7 cosine_reduce_fusion
  169.5 3.5 %collective-permute-done.14 = bf16[3,134,192]{1,2,0:T(8,128)(2,1)S(1)} collective-permute-done((bf16[3,134,192]{1,2,0:T(8,128)(2,1)S(1)}, bf16[3,134,192]{1,2,0:T(8,128)(2,1)S(1)}, u32[]{:S(2)}, u32[]{:S(2)}) %collective-permute-start.14) | collective-permute-done | bytes 154400 | tf_op jit(solution)/shard_map/ppermute | solution.py:18
  173.0 6.5 %collective-permute-done.15 = bf16[3,134,192]{1,2,0:T(8,128)(2,1)S(1)} collective-permute-done((bf16[3,134,192]{1,2,0:T(8,128)(2,1)S(1)}, bf16[3,134,192]{1,2,0:T(8,128)(2,1)S(1)}, u32[]{:S(2)}, u32[]{:S(2)}) %collective-permute-start.15) | collective-permute-done | bytes 154400 | tf_op jit(solution)/shard_map/ppermute | solution.py:17
  179.5 2.2 pad_maximum_fusion.3
  182.1 18.2 %fusion.31 = (f32[]{:T(128)}, f32[]{:T(128)}, f32[]{:T(128)}, f32[16,128,192]{1,2,0:T(8,128)}) fusion(f32[16,128,192]{1,2,0:T(8,128)S(1)} %copy-done.4, f32[16]{0:T(128)} %multiply_cosine_fusion, f32[16,128,192]{1,2,0:T(8,128)S(1)} %copy-done.2, f32[16,128,192]{1,2,0:T(8,128)S(1)} %copy-done.3, bf16[19,134,192]{1,2,0:T(8,128)(2,1)S(1)} %get-tuple-element.23, ...), kind=kLoop, calls=%fused_computation.80 | loop fusion | flops 68812800 | bytes 40182604 | tf_op jit(solution)/shard_map/reduce_sum | solution.py:77
  200.4 3.1 %all-reduce.1 = (f32[]{:T(128)}, f32[]{:T(128)}, f32[]{:T(128)}) all-reduce(f32[]{:T(128)} %get-tuple-element.11, f32[]{:T(128)} %get-tuple-element.12, f32[]{:T(128)} %get-tuple-element.10), channel_id=1, replica_groups=mesh['grp'=2,'lat'=8,'lon'=2] {'lon'}, use_global_device_ids=true, to_apply=%region_9.0 | all-reduce | flops 3 | bytes 24 | tf_op jit(solution)/shard_map/psum | solution.py:98
  203.5 20.6 %all-reduce = (f32[]{:T(128)}, f32[]{:T(128)}, f32[]{:T(128)}) all-reduce(f32[]{:T(128)} %get-tuple-element.16, f32[]{:T(128)} %get-tuple-element.17, f32[]{:T(128)} %get-tuple-element.18), channel_id=1, replica_groups=mesh['grp'=2,'lat'=8,'lon'=2] {'lat'}, use_global_device_ids=true, to_apply=%region_10.0 | all-reduce | flops 3 | bytes 24 | tf_op jit(solution)/shard_map/psum | solution.py:97
  226.1 2.8 %broadcast_divide_fusion = f32[16,128,192]{1,2,0:T(8,128)} fusion(f32[16,128,192]{1,2,0:T(8,128)} %get-tuple-element.19, f32[16]{0:T(128)S(1)} %broadcast_multiply_fusion.8), kind=kLoop, calls=%fused_computation.133 | loop fusion | flops 393216 | bytes 3145792 | tf_op jit(solution)/shard_map/div | solution.py:104
  (374 shorter events, 3.4 us)
Async XLA Ops:
  2.9 3.5 %collective-permute-start = (bf16[16,3,192]{2,0,1:T(8,128)(2,1)S(1)}, bf16[16,3,192]{2,0,1:T(8,128)(2,1)S(1)}, u32[]{:S(2)}, u32[]{:S(2)}) collective-permute-start(bf16[16,3,192]{2,0,1:T(8,128)(2,1)S(1)} %copy.14), channel_id=1, source_target_pairs={{0,1},{1,0},{2,3},{3,2},{4,5},{5,4},{6,7},{7,6},{8,9},{9,8},{10,11... | collective-permute-start | bytes 55304 | tf_op jit(solution)/shard_map/ppermute | solution.py:17
  3.8 3.0 %collective-permute-start.1 = (bf16[16,3,192]{2,0,1:T(8,128)(2,1)S(1)}, bf16[16,3,192]{2,0,1:T(8,128)(2,1)S(1)}, u32[]{:S(2)}, u32[]{:S(2)}) collective-permute-start(bf16[16,3,192]{2,0,1:T(8,128)(2,1)S(1)} %copy.15), channel_id=1, source_target_pairs={{1,0},{0,1},{3,2},{2,3},{5,4},{4,5},{7,6},{6,7},{9,8},{8,9},{11,10... | collective-permute-start | bytes 55304 | tf_op jit(solution)/shard_map/ppermute | solution.py:18
  4.1 50.5 %copy-start.9 = (f32[7,7,192]{2,1,0:T(8,128)}, f32[7,7,192]{2,1,0:T(8,128)S(1)}, u32[]{:S(2)}) copy-start(f32[7,7,192]{2,1,0:T(8,128)S(1)} %get-tuple-element.156) | copy-start | bytes 112900
  4.1 23.5 %copy-start.12 = (f32[1,1,192]{2,1,0:T(1,128)}, f32[1,1,192]{2,1,0:T(1,128)S(1)}, u32[]{:S(2)}) copy-start(f32[1,1,192]{2,1,0:T(1,128)S(1)} %get-tuple-element.116) | copy-start | bytes 2308
  4.1 23.5 %copy-start.14 = (f32[1,1,192]{2,1,0:T(1,128)}, f32[1,1,192]{2,1,0:T(1,128)S(1)}, u32[]{:S(2)}) copy-start(f32[1,1,192]{2,1,0:T(1,128)S(1)} %get-tuple-element.117) | copy-start | bytes 2308
  4.1 23.5 %copy-start.16 = (f32[1,1,192]{2,1,0:T(1,128)}, f32[1,1,192]{2,1,0:T(1,128)S(1)}, u32[]{:S(2)}) copy-start(f32[1,1,192]{2,1,0:T(1,128)S(1)} %get-tuple-element.118) | copy-start | bytes 2308
  4.1 23.5 %copy-start.18 = (f32[1,1,192]{2,1,0:T(1,128)}, f32[1,1,192]{2,1,0:T(1,128)S(1)}, u32[]{:S(2)}) copy-start(f32[1,1,192]{2,1,0:T(1,128)S(1)} %get-tuple-element.119) | copy-start | bytes 2308
  4.1 23.5 %copy-start.20 = (f32[1,1,192]{2,1,0:T(1,128)}, f32[1,1,192]{2,1,0:T(1,128)S(1)}, u32[]{:S(2)}) copy-start(f32[1,1,192]{2,1,0:T(1,128)S(1)} %get-tuple-element.120) | copy-start | bytes 2308
  4.1 23.5 %copy-start.22 = (f32[1,1,192]{2,1,0:T(1,128)}, f32[1,1,192]{2,1,0:T(1,128)S(1)}, u32[]{:S(2)}) copy-start(f32[1,1,192]{2,1,0:T(1,128)S(1)} %get-tuple-element.121) | copy-start | bytes 2308
  4.1 23.5 %copy-start.24 = (f32[1,1,192]{2,1,0:T(1,128)}, f32[1,1,192]{2,1,0:T(1,128)S(1)}, u32[]{:S(2)}) copy-start(f32[1,1,192]{2,1,0:T(1,128)S(1)} %get-tuple-element.122) | copy-start | bytes 2308
  4.2 23.5 %copy-start.26 = (f32[1,1,192]{2,1,0:T(1,128)}, f32[1,1,192]{2,1,0:T(1,128)S(1)}, u32[]{:S(2)}) copy-start(f32[1,1,192]{2,1,0:T(1,128)S(1)} %get-tuple-element.123) | copy-start | bytes 2308
  4.2 23.5 %copy-start.28 = (f32[1,1,192]{2,1,0:T(1,128)}, f32[1,1,192]{2,1,0:T(1,128)S(1)}, u32[]{:S(2)}) copy-start(f32[1,1,192]{2,1,0:T(1,128)S(1)} %get-tuple-element.124) | copy-start | bytes 2308
  4.2 23.5 %copy-start.30 = (f32[1,1,192]{2,1,0:T(1,128)}, f32[1,1,192]{2,1,0:T(1,128)S(1)}, u32[]{:S(2)}) copy-start(f32[1,1,192]{2,1,0:T(1,128)S(1)} %get-tuple-element.125) | copy-start | bytes 2308
  4.2 23.5 %copy-start.32 = (f32[1,1,192]{2,1,0:T(1,128)}, f32[1,1,192]{2,1,0:T(1,128)S(1)}, u32[]{:S(2)}) copy-start(f32[1,1,192]{2,1,0:T(1,128)S(1)} %get-tuple-element.126) | copy-start | bytes 2308
  4.2 23.5 %copy-start.34 = (f32[1,1,192]{2,1,0:T(1,128)}, f32[1,1,192]{2,1,0:T(1,128)S(1)}, u32[]{:S(2)}) copy-start(f32[1,1,192]{2,1,0:T(1,128)S(1)} %get-tuple-element.127) | copy-start | bytes 2308
  4.2 23.5 %copy-start.36 = (f32[1,1,192]{2,1,0:T(1,128)}, f32[1,1,192]{2,1,0:T(1,128)S(1)}, u32[]{:S(2)}) copy-start(f32[1,1,192]{2,1,0:T(1,128)S(1)} %get-tuple-element.128) | copy-start | bytes 2308
  4.2 23.5 %copy-start.38 = (f32[1,1,192]{2,1,0:T(1,128)}, f32[1,1,192]{2,1,0:T(1,128)S(1)}, u32[]{:S(2)}) copy-start(f32[1,1,192]{2,1,0:T(1,128)S(1)} %get-tuple-element.129) | copy-start | bytes 2308
  4.2 23.5 %copy-start.40 = (f32[1,1,192]{2,1,0:T(1,128)}, f32[1,1,192]{2,1,0:T(1,128)S(1)}, u32[]{:S(2)}) copy-start(f32[1,1,192]{2,1,0:T(1,128)S(1)} %get-tuple-element.130) | copy-start | bytes 2308
  4.2 23.5 %copy-start.42 = (f32[1,1,192]{2,1,0:T(1,128)}, f32[1,1,192]{2,1,0:T(1,128)S(1)}, u32[]{:S(2)}) copy-start(f32[1,1,192]{2,1,0:T(1,128)S(1)} %get-tuple-element.131) | copy-start | bytes 2308
  4.2 23.5 %copy-start.44 = (f32[1,1,192]{2,1,0:T(1,128)}, f32[1,1,192]{2,1,0:T(1,128)S(1)}, u32[]{:S(2)}) copy-start(f32[1,1,192]{2,1,0:T(1,128)S(1)} %get-tuple-element.132) | copy-start | bytes 2308
  4.3 23.5 %copy-start.46 = (f32[1,1,192]{2,1,0:T(1,128)}, f32[1,1,192]{2,1,0:T(1,128)S(1)}, u32[]{:S(2)}) copy-start(f32[1,1,192]{2,1,0:T(1,128)S(1)} %get-tuple-element.133) | copy-start | bytes 2308
  4.3 23.5 %copy-start.48 = (f32[1,1,192]{2,1,0:T(1,128)}, f32[1,1,192]{2,1,0:T(1,128)S(1)}, u32[]{:S(2)}) copy-start(f32[1,1,192]{2,1,0:T(1,128)S(1)} %get-tuple-element.134) | copy-start | bytes 2308
  4.3 23.4 %copy-start.50 = (f32[1,1,192]{2,1,0:T(1,128)}, f32[1,1,192]{2,1,0:T(1,128)S(1)}, u32[]{:S(2)}) copy-start(f32[1,1,192]{2,1,0:T(1,128)S(1)} %get-tuple-element.97) | copy-start | bytes 2308
  4.3 23.4 %copy-start.52 = (f32[1,1,192]{2,1,0:T(1,128)}, f32[1,1,192]{2,1,0:T(1,128)S(1)}, u32[]{:S(2)}) copy-start(f32[1,1,192]{2,1,0:T(1,128)S(1)} %get-tuple-element.98) | copy-start | bytes 2308
  4.3 23.4 %copy-start.54 = (f32[1,1,192]{2,1,0:T(1,128)}, f32[1,1,192]{2,1,0:T(1,128)S(1)}, u32[]{:S(2)}) copy-start(f32[1,1,192]{2,1,0:T(1,128)S(1)} %get-tuple-element.99) | copy-start | bytes 2308
  4.3 23.4 %copy-start.56 = (f32[1,1,192]{2,1,0:T(1,128)}, f32[1,1,192]{2,1,0:T(1,128)S(1)}, u32[]{:S(2)}) copy-start(f32[1,1,192]{2,1,0:T(1,128)S(1)} %get-tuple-element.100) | copy-start | bytes 2308
  4.3 23.4 %copy-start.58 = (f32[1,1,192]{2,1,0:T(1,128)}, f32[1,1,192]{2,1,0:T(1,128)S(1)}, u32[]{:S(2)}) copy-start(f32[1,1,192]{2,1,0:T(1,128)S(1)} %get-tuple-element.101) | copy-start | bytes 2308
  4.4 23.4 %copy-start.60 = (f32[1,1,192]{2,1,0:T(1,128)}, f32[1,1,192]{2,1,0:T(1,128)S(1)}, u32[]{:S(2)}) copy-start(f32[1,1,192]{2,1,0:T(1,128)S(1)} %get-tuple-element.102) | copy-start | bytes 2308
  4.4 23.4 %copy-start.62 = (f32[1,1,192]{2,1,0:T(1,128)}, f32[1,1,192]{2,1,0:T(1,128)S(1)}, u32[]{:S(2)}) copy-start(f32[1,1,192]{2,1,0:T(1,128)S(1)} %get-tuple-element.103) | copy-start | bytes 2308
  4.4 23.4 %copy-start.64 = (f32[1,1,192]{2,1,0:T(1,128)}, f32[1,1,192]{2,1,0:T(1,128)S(1)}, u32[]{:S(2)}) copy-start(f32[1,1,192]{2,1,0:T(1,128)S(1)} %get-tuple-element.104) | copy-start | bytes 2308
  4.4 23.4 %copy-start.66 = (f32[1,1,192]{2,1,0:T(1,128)}, f32[1,1,192]{2,1,0:T(1,128)S(1)}, u32[]{:S(2)}) copy-start(f32[1,1,192]{2,1,0:T(1,128)S(1)} %get-tuple-element.105) | copy-start | bytes 2308
  4.4 23.4 %copy-start.68 = (f32[1,1,192]{2,1,0:T(1,128)}, f32[1,1,192]{2,1,0:T(1,128)S(1)}, u32[]{:S(2)}) copy-start(f32[1,1,192]{2,1,0:T(1,128)S(1)} %get-tuple-element.106) | copy-start | bytes 2308
  4.4 23.4 %copy-start.70 = (f32[1,1,192]{2,1,0:T(1,128)}, f32[1,1,192]{2,1,0:T(1,128)S(1)}, u32[]{:S(2)}) copy-start(f32[1,1,192]{2,1,0:T(1,128)S(1)} %get-tuple-element.107) | copy-start | bytes 2308
  4.4 23.4 %copy-start.72 = (f32[1,1,192]{2,1,0:T(1,128)}, f32[1,1,192]{2,1,0:T(1,128)S(1)}, u32[]{:S(2)}) copy-start(f32[1,1,192]{2,1,0:T(1,128)S(1)} %get-tuple-element.108) | copy-start | bytes 2308
  4.4 23.4 %copy-start.74 = (f32[1,1,192]{2,1,0:T(1,128)}, f32[1,1,192]{2,1,0:T(1,128)S(1)}, u32[]{:S(2)}) copy-start(f32[1,1,192]{2,1,0:T(1,128)S(1)} %get-tuple-element.109) | copy-start | bytes 2308
  4.4 23.4 %copy-start.76 = (f32[1,1,192]{2,1,0:T(1,128)}, f32[1,1,192]{2,1,0:T(1,128)S(1)}, u32[]{:S(2)}) copy-start(f32[1,1,192]{2,1,0:T(1,128)S(1)} %get-tuple-element.110) | copy-start | bytes 2308
  4.4 23.4 %copy-start.78 = (f32[1,1,192]{2,1,0:T(1,128)}, f32[1,1,192]{2,1,0:T(1,128)S(1)}, u32[]{:S(2)}) copy-start(f32[1,1,192]{2,1,0:T(1,128)S(1)} %get-tuple-element.111) | copy-start | bytes 2308
  4.5 23.4 %copy-start.80 = (f32[1,1,192]{2,1,0:T(1,128)}, f32[1,1,192]{2,1,0:T(1,128)S(1)}, u32[]{:S(2)}) copy-start(f32[1,1,192]{2,1,0:T(1,128)S(1)} %get-tuple-element.112) | copy-start | bytes 2308
  4.5 23.4 %copy-start.82 = (f32[1,1,192]{2,1,0:T(1,128)}, f32[1,1,192]{2,1,0:T(1,128)S(1)}, u32[]{:S(2)}) copy-start(f32[1,1,192]{2,1,0:T(1,128)S(1)} %get-tuple-element.113) | copy-start | bytes 2308
  4.5 23.4 %copy-start.84 = (f32[1,1,192]{2,1,0:T(1,128)}, f32[1,1,192]{2,1,0:T(1,128)S(1)}, u32[]{:S(2)}) copy-start(f32[1,1,192]{2,1,0:T(1,128)S(1)} %get-tuple-element.114) | copy-start | bytes 2308
  4.5 23.4 %copy-start.86 = (f32[1,1,192]{2,1,0:T(1,128)}, f32[1,1,192]{2,1,0:T(1,128)S(1)}, u32[]{:S(2)}) copy-start(f32[1,1,192]{2,1,0:T(1,128)S(1)} %get-tuple-element.115) | copy-start | bytes 2308
  7.7 17.6 %collective-permute-start.2 = (bf16[3,134,192]{1,2,0:T(8,128)(2,1)S(1)}, bf16[3,134,192]{1,2,0:T(8,128)(2,1)S(1)}, u32[]{:S(2)}, u32[]{:S(2)}) collective-permute-start(bf16[3,134,192]{1,2,0:T(8,128)(2,1)S(1)} %get-tuple-element.36), channel_id=1, source_target_pairs={{0,2},{2,4},{4,6},{6,8},{8,10},{10,12},{12,14},{1,3},{3,5},{5,7},{... | collective-permute-start | bytes 463112 | tf_op jit(solution)/shard_map/ppermute | solution.py:17
  12.6 12.7 %collective-permute-start.3 = (bf16[3,134,192]{1,2,0:T(8,128)(2,1)S(1)}, bf16[3,134,192]{1,2,0:T(8,128)(2,1)S(1)}, u32[]{:S(2)}, u32[]{:S(2)}) collective-permute-start(bf16[3,134,192]{1,2,0:T(8,128)(2,1)S(1)} %get-tuple-element.37), channel_id=1, source_target_pairs={{2,0},{4,2},{6,4},{8,6},{10,8},{12,10},{14,12},{3,1},{5,3},{7,5},{... | collective-permute-start | bytes 463112 | tf_op jit(solution)/shard_map/ppermute | solution.py:18
  53.5 1.7 collective-permute-start.4
  54.0 1.7 collective-permute-start.5
  56.4 17.2 %collective-permute-start.6 = (bf16[3,134,192]{1,2,0:T(8,128)(2,1)S(1)}, bf16[3,134,192]{1,2,0:T(8,128)(2,1)S(1)}, u32[]{:S(2)}, u32[]{:S(2)}) collective-permute-start(bf16[3,134,192]{1,2,0:T(8,128)(2,1)S(1)} %get-tuple-element.32), channel_id=1, source_target_pairs={{0,2},{2,4},{4,6},{6,8},{8,10},{10,12},{12,14},{1,3},{3,5},{5,7},{... | collective-permute-start | bytes 463112 | tf_op jit(solution)/shard_map/ppermute | solution.py:17
  60.9 12.8 %collective-permute-start.7 = (bf16[3,134,192]{1,2,0:T(8,128)(2,1)S(1)}, bf16[3,134,192]{1,2,0:T(8,128)(2,1)S(1)}, u32[]{:S(2)}, u32[]{:S(2)}) collective-permute-start(bf16[3,134,192]{1,2,0:T(8,128)(2,1)S(1)} %get-tuple-element.33), channel_id=1, source_target_pairs={{2,0},{4,2},{6,4},{8,6},{10,8},{12,10},{14,12},{3,1},{5,3},{7,5},{... | collective-permute-start | bytes 463112 | tf_op jit(solution)/shard_map/ppermute | solution.py:18
  108.4 1.3 collective-permute-start.8
  108.8 1.4 collective-permute-start.9
  111.0 11.9 %collective-permute-start.10 = (bf16[3,134,192]{1,2,0:T(8,128)(2,1)S(1)}, bf16[3,134,192]{1,2,0:T(8,128)(2,1)S(1)}, u32[]{:S(2)}, u32[]{:S(2)}) collective-permute-start(bf16[3,134,192]{1,2,0:T(8,128)(2,1)S(1)} %get-tuple-element.28), channel_id=1, source_target_pairs={{2,0},{4,2},{6,4},{8,6},{10,8},{12,10},{14,12},{3,1},{5,3},{7,5},{... | collective-permute-start | bytes 463112 | tf_op jit(solution)/shard_map/ppermute | solution.py:18
  112.3 20.0 %copy-start.1 = (f32[16,128,192]{1,2,0:T(8,128)S(1)}, f32[16,128,192]{1,2,0:T(8,128)}, u32[]{:S(2)}) copy-start(f32[16,128,192]{1,2,0:T(8,128)} %copy-done) | copy-start | bytes 4718596
  112.3 20.0 %copy-start.88 = (f32[1,1,192]{2,1,0:T(1,128)S(1)}, f32[1,1,192]{2,1,0:T(1,128)}, u32[]{:S(2)}) copy-start(f32[1,1,192]{2,1,0:T(1,128)} %get-tuple-element.48) | copy-start | bytes 2308
  112.3 20.0 %copy-start.90 = (f32[1,1,192]{2,1,0:T(1,128)S(1)}, f32[1,1,192]{2,1,0:T(1,128)}, u32[]{:S(2)}) copy-start(f32[1,1,192]{2,1,0:T(1,128)} %get-tuple-element.49) | copy-start | bytes 2308
  112.4 20.0 %copy-start.92 = (f32[1,1,192]{2,1,0:T(1,128)S(1)}, f32[1,1,192]{2,1,0:T(1,128)}, u32[]{:S(2)}) copy-start(f32[1,1,192]{2,1,0:T(1,128)} %get-tuple-element.50) | copy-start | bytes 2308
  112.4 20.0 %copy-start.94 = (f32[1,1,192]{2,1,0:T(1,128)S(1)}, f32[1,1,192]{2,1,0:T(1,128)}, u32[]{:S(2)}) copy-start(f32[1,1,192]{2,1,0:T(1,128)} %get-tuple-element.51) | copy-start | bytes 2308
  112.4 20.0 %copy-start.96 = (f32[1,1,192]{2,1,0:T(1,128)S(1)}, f32[1,1,192]{2,1,0:T(1,128)}, u32[]{:S(2)}) copy-start(f32[1,1,192]{2,1,0:T(1,128)} %get-tuple-element.52) | copy-start | bytes 2308
  112.4 20.0 %copy-start.98 = (f32[1,1,192]{2,1,0:T(1,128)S(1)}, f32[1,1,192]{2,1,0:T(1,128)}, u32[]{:S(2)}) copy-start(f32[1,1,192]{2,1,0:T(1,128)} %get-tuple-element.53) | copy-start | bytes 2308
  112.4 20.0 %copy-start.100 = (f32[1,1,192]{2,1,0:T(1,128)S(1)}, f32[1,1,192]{2,1,0:T(1,128)}, u32[]{:S(2)}) copy-start(f32[1,1,192]{2,1,0:T(1,128)} %get-tuple-element.54) | copy-start | bytes 2308
  112.4 20.0 %copy-start.102 = (f32[1,1,192]{2,1,0:T(1,128)S(1)}, f32[1,1,192]{2,1,0:T(1,128)}, u32[]{:S(2)}) copy-start(f32[1,1,192]{2,1,0:T(1,128)} %get-tuple-element.55) | copy-start | bytes 2308
  112.7 17.4 %collective-permute-start.11 = (bf16[3,134,192]{1,2,0:T(8,128)(2,1)S(1)}, bf16[3,134,192]{1,2,0:T(8,128)(2,1)S(1)}, u32[]{:S(2)}, u32[]{:S(2)}) collective-permute-start(bf16[3,134,192]{1,2,0:T(8,128)(2,1)S(1)} %get-tuple-element.29), channel_id=1, source_target_pairs={{0,2},{2,4},{4,6},{6,8},{8,10},{10,12},{12,14},{1,3},{3,5},{5,7},{... | collective-permute-start | bytes 463112 | tf_op jit(solution)/shard_map/ppermute | solution.py:17
  158.5 1.3 collective-permute-start.12
  158.9 1.4 collective-permute-start.13
  161.1 11.9 %collective-permute-start.14 = (bf16[3,134,192]{1,2,0:T(8,128)(2,1)S(1)}, bf16[3,134,192]{1,2,0:T(8,128)(2,1)S(1)}, u32[]{:S(2)}, u32[]{:S(2)}) collective-permute-start(bf16[3,134,192]{1,2,0:T(8,128)(2,1)S(1)} %get-tuple-element.24), channel_id=1, source_target_pairs={{2,0},{4,2},{6,4},{8,6},{10,8},{12,10},{14,12},{3,1},{5,3},{7,5},{... | collective-permute-start | bytes 463112 | tf_op jit(solution)/shard_map/ppermute | solution.py:18
  162.4 17.1 %collective-permute-start.15 = (bf16[3,134,192]{1,2,0:T(8,128)(2,1)S(1)}, bf16[3,134,192]{1,2,0:T(8,128)(2,1)S(1)}, u32[]{:S(2)}, u32[]{:S(2)}) collective-permute-start(bf16[3,134,192]{1,2,0:T(8,128)(2,1)S(1)} %get-tuple-element.25), channel_id=1, source_target_pairs={{0,2},{2,4},{4,6},{6,8},{8,10},{10,12},{12,14},{1,3},{3,5},{5,7},{... | collective-permute-start | bytes 463112 | tf_op jit(solution)/shard_map/ppermute | solution.py:17
  (123 other events, 1662.3 us)
